TPU v7x, 128 devices: a whole 4x4x4 slice. The times are simulated.
128 devices in a mesh: gx: 8 (over y, z_hi), gy: 16 (over z_lo, x, core).
Axes of the slice: x: 4, y: 4, z: 4 (z_hi: 2, z_lo: 2; z = z_hi * 2 + z_lo), core: 2. Of those that a mesh axis runs over, the one named last changes fastest.
Arguments:
- saved_conc: float32 [3, 2, 64, 128, 1024], P(None, None, None, 'gy', 'gx'), may hold values from 0.15 to 0.85
- adjoint_end: float32 [2, 64, 128, 1024], P(None, None, 'gy', 'gx'), may hold values from -6 to 6
- rate_field: float32 [64, 128, 1024], P(None, 'gy', 'gx'), may hold values from 0.5 to 5
Outputs:
- adjoint_start: float32 [2, 64, 128, 1024], P(None, None, 'gy', 'gx')
- rate_grad: float32 [64, 128, 1024], P(None, 'gy', 'gx')
All inputs are finite; a program needn't handle non-finite values.
Results may differ from a plain program's by a relative error of at most 0.00023.
Values sent between devices are 32-bit elements; how exact they have to be, the bound alone decides.
A program may use at most 128 MiB of HBM per device.

v0:
```python
import jax
import jax.numpy as jnp
from jax import lax
from jax.experimental import pallas as pl
from jax.experimental.pallas import tpu as pltpu
from jax.sharding import PartitionSpec as P

MESH = pl.DeviceIdType.MESH
DIRS = ((1, 0), (-1, 0), (0, 1), (0, -1), (1, 1), (1, -1), (-1, 1), (-1, -1))
ADJ, RATE, C, NEXT = 0, 2, (4, 3, 1), (0, 5, 6)
HALO, PAD = 2, 16


def body(sizes, conc_hbm, adj_hbm, rate_hbm, out_hbm, grad_hbm,
         raw, raw_rate, field, mob, pot, inv, gpot, part, acc, outs,
         load_sem, store_sem, send_sem, recv_sem):
    ngx, ngy, rows, cols, depth = sizes
    gx, gy = lax.axis_index("gx"), lax.axis_index("gy")
    lo, hi = HALO, HALO + rows
    xl, xh = PAD, PAD + cols

    def device(dy, dx):
        return (lax.rem(gx + dx + ngx, ngx), lax.rem(gy + dy + ngy, ngy))

    barrier = pltpu.get_barrier_semaphore()
    for dy, dx in DIRS:
        pl.semaphore_signal(barrier, inc=1, device_id=device(dy, dx), device_id_type=MESH)

    loads = []
    for slot, src in enumerate((adj_hbm, conc_hbm.at[2], rate_hbm, conc_hbm.at[1], conc_hbm.at[0])):
        group = []
        for y in range(rows):
            dst = raw_rate.at[y] if slot == RATE else raw.at[slot, y]
            group.append(pltpu.make_async_copy(src.at[:, y, :], dst, load_sem.at[slot, y]))
            group[-1].start()
        loads.append(group)

    def flip(slot):
        for y in range(rows):
            loads[slot][y].wait()
            if slot == RATE:
                half = (0.1 * raw_rate[y]).T
                tile = jnp.concatenate([half, half], axis=-1)
            else:
                tile = raw[slot, y].T
            field[slot, lo + y, xl:xh, :] = tile

    lane = lax.broadcasted_iota(jnp.int32, (8, 128), 1)
    upper = lax.rem(lane, depth) != depth - 1

    def mask(v):
        keep = jnp.broadcast_to(upper[:1], v.shape)
        return jnp.where(keep, v, 0.0)

    def up(v):
        return pltpu.roll(v, 127, 1)

    def down(v):
        return pltpu.roll(v, 1, 1)

    def laplace(ref, index, y, x, n):
        v = ref[(*index, y, pl.ds(x, n))]
        sides = (ref[(*index, y, pl.ds(x - 1, n))] + ref[(*index, y, pl.ds(x + 1, n))]
                 + ref[(*index, y - 1, pl.ds(x, n))] + ref[(*index, y + 1, pl.ds(x, n))])
        step = mask(up(v) - v)
        return v, sides - 4.0 * v + (step - down(step))

    def mobility(n, y, pieces):
        for x, w in pieces:
            c = field[C[n], y, pl.ds(x, w)]
            mob[n, y, pl.ds(x, w)] = c * (1.0 - c)

    def chem(n, y, pieces):
        for x, w in pieces:
            c, lap = laplace(field, (C[n],), y, x, w)
            m = c * (1.0 - c)
            r = 1.0 / m
            mob[n, y, pl.ds(x, w)] = m
            inv[n, y, pl.ds(x, w)] = r
            pot[n, y, pl.ds(x, w)] = jnp.log(c * c * r) + 2.5 * (1.0 - 2.0 * c) - lap

    def gflux(n, y, pieces):
        src = NEXT[2 - n]
        for x, w in pieces:
            b, m, u = field[src, y, pl.ds(x, w)], mob[n, y, pl.ds(x, w)], pot[n, y, pl.ds(x, w)]
            step = mask(up(b) - b)
            flux = (up(m) + m) * step
            term = (up(u) - u) * step
            g, q = flux - down(flux), term + down(term)
            for dy, dx in ((0, 1), (0, -1), (1, 0), (-1, 0)):
                at = (y + dy, pl.ds(x + dx, w))
                d = field[(src, *at)] - b
                g = g + (mob[(n, *at)] + m) * d
                q = q + (pot[(n, *at)] - u) * d
            g = 0.015 * g - field[RATE, y, pl.ds(x, w)] * b
            gpot[y, pl.ds(x, w)] = g
            c = field[C[n], y, pl.ds(x, w)]
            part[y, pl.ds(x, w)] = b - (0.015 * (1.0 - 2.0 * c)) * q + (inv[n, y, pl.ds(x, w)] - 5.0) * g

    def update(n, y, pieces):
        for x, w in pieces:
            _, lap = laplace(gpot, (), y, x, w)
            new = part[y, pl.ds(x, w)] - lap
            if n == 0:
                acc[1, y - lo, pl.ds(x - xl, w)] = new
            else:
                field[NEXT[3 - n], y, pl.ds(x, w)] = new

    def grad(n, y, _):
        for x in range(0, cols, 64):
            s = field[NEXT[2 - n], y, pl.ds(xl + x, 64)] * (0.5 - pot[n, y, pl.ds(xl + x, 64)])
            if n < 2:
                s = s + acc[0, y - lo, pl.ds(x, 64)]
            acc[0, y - lo, pl.ds(x, 64)] = s

    FULL = ((8, 48), (56, 48), (104, 48))
    OWN = ((16, 64), (80, 64))
    INNER = ((17, 64), (79, 64))
    CORE = ((18, 64), (78, 64))
    MAIN = ((24, 56), (80, 56))
    WIDE = ((8, 16), (136, 16))
    EDGE = ((16, 8), (136, 8))

    def rows_of(fn, n, first, count, pieces, gap=0):
        def one(k, _):
            fn(n, first + k + (gap * (k // (count // 2)) if gap else 0), pieces)
            return 0
        lax.fori_loop(0, count, one, 0)

    def message(which, k, fields, dy, dx, width, sem):
        ys = {1: (hi - width, lo - width), -1: (lo, hi), 0: (lo, lo)}[dy]
        xs = {1: (xh - HALO, xl - HALO), -1: (xl, xh), 0: (xl, xl)}[dx]
        h = rows if dy == 0 else width
        w = cols if dx == 0 else HALO
        f = pl.ds(*fields)
        return pltpu.make_async_remote_copy(
            src_ref=field.at[f, pl.ds(ys[0], h), pl.ds(xs[0], w)],
            dst_ref=field.at[f, pl.ds(ys[1], h), pl.ds(xs[1], w)],
            send_sem=send_sem.at[sem], recv_sem=recv_sem.at[sem],
            device_id=device(dy, dx), device_id_type=MESH)

    for slot in range(5):
        flip(slot)
    for n in (2, 1, 0):
        rows_of(mobility, n, lo, 1, OWN)
        rows_of(mobility, n, hi - 1, 1, OWN)
        rows_of(chem, n, lo + 1, rows - 2, INNER)

    pl.semaphore_wait(barrier, len(DIRS))
    first = []
    for k, (dy, dx) in enumerate(DIRS):
        if dx == 0:
            first.append(message(0, k, (0, 2), dy, dx, 2, k))
            first.append(message(0, k, (2, 1), dy, dx, 1, 8 + k))
        else:
            first.append(message(0, k, (0, 3), dy, dx, 2, k))
    later = [message(1, k, (3, 2), dy, dx, 2, 16 + k) for k, (dy, dx) in enumerate(DIRS)]
    for copy in first + later:
        copy.start()

    def before(n):
        rows_of(gflux, n, lo + 1, rows - 2, CORE)
        rows_of(update, n, lo + 2, rows - 4, MAIN)

    def rim(n):
        rows_of(mobility, n, lo - 2, 1, FULL)
        rows_of(mobility, n, hi + 1, 1, FULL)
        rows_of(chem, n, lo - 1, 4, FULL, 6)
        rows_of(chem, n, lo + 1, rows - 2, WIDE)

    def after(n):
        if n == 2:
            rows_of(gflux, n, lo - 1, 6, FULL, 4)
        else:
            rows_of(gflux, n, lo - 1, 4, FULL, 6)
        rows_of(gflux, n, lo + 1, rows - 2, WIDE)
        rows_of(update, n, lo, 4, OWN, 4)
        rows_of(update, n, lo + 2, rows - 4, EDGE)

    before(2)
    for copy in first:
        copy.wait_recv()
    rim(2)
    after(2)
    second = [message(2, k, (5, 1), dy, dx, 2, 24 + k) for k, (dy, dx) in enumerate(DIRS)]
    for copy in second:
        copy.start()
    rows_of(grad, 2, lo, rows, ())
    for copy in later:
        copy.wait_recv()
    rim(1)
    before(1)
    rim(0)
    rows_of(grad, 1, lo, rows, ())
    for copy in second:
        copy.wait_recv()
    after(1)
    third = [message(3, k, (6, 1), dy, dx, 2, 32 + k) for k, (dy, dx) in enumerate(DIRS)]
    for copy in third:
        copy.start()
    before(0)
    rows_of(grad, 0, lo, rows, ())
    stores = []
    for y in range(rows):
        s = acc[0, y]
        s = 0.1 * (s + pltpu.roll(s, depth, 1))
        outs[0, y] = s.T
        stores.append(pltpu.make_async_copy(outs.at[0, y, pl.ds(0, depth)], grad_hbm.at[:, y, :], store_sem.at[0, y]))
        stores[-1].start()
    for copy in third:
        copy.wait_recv()
    after(0)
    for y in range(rows):
        outs[1, y] = acc[1, y].T
        stores.append(pltpu.make_async_copy(outs.at[1, y], out_hbm.at[:, y, :], store_sem.at[1, y]))
        stores[-1].start()
    for copy in first + later + second + third:
        copy.wait_send()
    for copy in stores:
        copy.wait()


def solution(mesh):
    ngx, ngy = mesh.shape["gx"], mesh.shape["gy"]

    def shards(saved_conc, adjoint_end, rate_field):
        steps, frames, depth, rows, cols = saved_conc.shape
        lanes = frames * depth
        conc = saved_conc.reshape(steps, lanes, rows, cols)
        adj = adjoint_end.reshape(lanes, rows, cols)
        ext = (rows + 2 * HALO, cols + 2 * PAD, lanes)

        def kernel(*refs):
            body((ngx, ngy, rows, cols, depth), *refs)

        hbm = pl.BlockSpec(memory_space=pl.ANY)
        out, grad = pl.pallas_call(
            kernel,
            out_shape=(jax.ShapeDtypeStruct((lanes, rows, cols), jnp.float32),
                       jax.ShapeDtypeStruct((depth, rows, cols), jnp.float32)),
            in_specs=[hbm] * 3, out_specs=(hbm, hbm),
            scratch_shapes=[
                pltpu.VMEM((5, rows, lanes, cols), jnp.float32),
                pltpu.VMEM((rows, depth, cols), jnp.float32),
                pltpu.VMEM((7, *ext), jnp.float32),
                pltpu.VMEM((3, *ext), jnp.float32),
                pltpu.VMEM((3, *ext), jnp.float32),
                pltpu.VMEM((3, *ext), jnp.float32),
                pltpu.VMEM(ext, jnp.float32),
                pltpu.VMEM(ext, jnp.float32),
                pltpu.VMEM((2, rows, cols, lanes), jnp.float32),
                pltpu.VMEM((2, rows, lanes, cols), jnp.float32),
                pltpu.SemaphoreType.DMA((5, rows)),
                pltpu.SemaphoreType.DMA((2, rows)),
                pltpu.SemaphoreType.DMA((40,)),
                pltpu.SemaphoreType.DMA((40,)),
            ],
            compiler_params=pltpu.CompilerParams(
                collective_id=0, has_side_effects=True, vmem_limit_bytes=56 << 20),
        )(conc, adj, rate_field)
        return out.reshape(adjoint_end.shape), grad

    return jax.shard_map(
        shards, mesh=mesh,
        in_specs=(P(None, None, None, "gy", "gx"), P(None, None, "gy", "gx"), P(None, "gy", "gx")),
        out_specs=(P(None, None, "gy", "gx"), P(None, "gy", "gx")),
        check_vma=False)
```

profile of v0, /device:TPU:0, one launch (start us, length us, event | category | flops | bytes accessed | tf_op | source)
XLA Modules:
  0.0 51.8 jit_solution(5074374029260645161)
XLA Ops:
  0.6 47.7 %shard_map.50 = (f32[128,8,128]{2,1,0:T(8,128)}, f32[64,8,128]{2,1,0:T(8,128)}) custom-call(f32[3,128,8,128]{3,2,1,0:T(8,128)} %bitcast.3, f32[128,8,128]{2,1,0:T(8,128)} %bitcast.5, f32[64,8,128]{2,1,0:T(8,128)} %refs_2_.1), custom_call_target="tpu_custom_call" | custom-call | tf_op jit(solution)/shard_map/pallas_call | solution.py:237
  48.3 1.9 %copy.7 = f32[2,64,8,128]{3,2,1,0:T(8,128)} copy(f32[2,64,8,128]{3,2,1,0:T(8,128)} %bitcast.4) | data formatting | bytes 1048576
  50.2 1.7 %copy.8 = f32[64,8,128]{2,1,0:T(8,128)} copy(f32[64,8,128]{2,1,0:T(8,128)} %get-tuple-element.9) | data formatting | bytes 524288
where the time goes:
time: 52.5 us; the launch traced here: 51.8 us
  Pallas kernels  47.7 us (91%)
  local copies, waits for them, and re-layouts  3.54 us (7%)
  between operations  0.64 us (1%)
    pallas_call x1, Pallas kernels, shards(): pl.pallas_call(kernel, out_shape=(jax.ShapeDtypeStruct((lanes, rows, cols...  47.7 us
    unnamed x2, local copies, waits for them, and re-layouts  3.54 us

commit v1 on v0

--- a/solution.py
+++ b/solution.py
@@ -6,8 +6,9 @@
 from jax.sharding import PartitionSpec as P
 
 MESH = pl.DeviceIdType.MESH
-DIRS = ((1, 0), (-1, 0), (0, 1), (0, -1), (1, 1), (1, -1), (-1, 1), (-1, -1))
+DIRS = ((1, 1), (1, -1), (-1, 1), (-1, -1), (0, 1), (0, -1), (1, 0), (-1, 0))
 ADJ, RATE, C, NEXT = 0, 2, (4, 3, 1), (0, 5, 6)
+UNROLL = (4, 3, 2, 1)
 HALO, PAD = 2, 16
 
 
@@ -46,11 +47,10 @@
             field[slot, lo + y, xl:xh, :] = tile
 
     lane = lax.broadcasted_iota(jnp.int32, (8, 128), 1)
-    upper = lax.rem(lane, depth) != depth - 1
-
-    def mask(v):
-        keep = jnp.broadcast_to(upper[:1], v.shape)
-        return jnp.where(keep, v, 0.0)
+    upper, lower = lax.rem(lane, depth) != depth - 1, lax.rem(lane, depth) != 0
+
+    def pick(keep, v, other):
+        return jnp.where(jnp.broadcast_to(keep[:1], v.shape), v, other)
 
     def up(v):
         return pltpu.roll(v, 127, 1)
@@ -62,8 +62,7 @@
         v = ref[(*index, y, pl.ds(x, n))]
         sides = (ref[(*index, y, pl.ds(x - 1, n))] + ref[(*index, y, pl.ds(x + 1, n))]
                  + ref[(*index, y - 1, pl.ds(x, n))] + ref[(*index, y + 1, pl.ds(x, n))])
-        step = mask(up(v) - v)
-        return v, sides - 4.0 * v + (step - down(step))
+        return v, sides - 6.0 * v + (pick(upper, up(v), v) + pick(lower, down(v), v))
 
     def mobility(n, y, pieces):
         for x, w in pieces:
@@ -83,7 +82,7 @@
         src = NEXT[2 - n]
         for x, w in pieces:
             b, m, u = field[src, y, pl.ds(x, w)], mob[n, y, pl.ds(x, w)], pot[n, y, pl.ds(x, w)]
-            step = mask(up(b) - b)
+            step = pick(upper, up(b) - b, 0.0)
             flux = (up(m) + m) * step
             term = (up(u) - u) * step
             g, q = flux - down(flux), term + down(term)
@@ -113,25 +112,34 @@
                 s = s + acc[0, y - lo, pl.ds(x, 64)]
             acc[0, y - lo, pl.ds(x, 64)] = s
 
-    FULL = ((8, 48), (56, 48), (104, 48))
-    OWN = ((16, 64), (80, 64))
+    FULL = ((8, 144),)
+    OWN = ((16, 128),)
     INNER = ((17, 64), (79, 64))
     CORE = ((18, 64), (78, 64))
-    MAIN = ((24, 56), (80, 56))
+    MAIN = ((24, 112),)
     WIDE = ((8, 16), (136, 16))
     EDGE = ((16, 8), (136, 8))
 
     def rows_of(fn, n, first, count, pieces, gap=0):
-        def one(k, _):
-            fn(n, first + k + (gap * (k // (count // 2)) if gap else 0), pieces)
+        step = next(u for u in UNROLL if count % u == 0)
+
+        def some(k, _):
+            for i in range(step):
+                r = k * step + i
+                fn(n, first + r + (gap * (r // (count // 2)) if gap else 0), pieces)
             return 0
-        lax.fori_loop(0, count, one, 0)
-
-    def message(which, k, fields, dy, dx, width, sem):
-        ys = {1: (hi - width, lo - width), -1: (lo, hi), 0: (lo, lo)}[dy]
-        xs = {1: (xh - HALO, xl - HALO), -1: (xl, xh), 0: (xl, xl)}[dx]
-        h = rows if dy == 0 else width
-        w = cols if dx == 0 else HALO
+
+        if step == count:
+            some(0, 0)
+        else:
+            lax.fori_loop(0, count // step, some, 0)
+
+    def message(fields, dy, dx, sem, ring=HALO):
+        ring = 1 if dy and dx else ring
+        ys = {1: (hi - ring, lo - ring), -1: (lo, hi), 0: (lo, lo)}[dy]
+        xs = {1: (xh - ring, xl - ring), -1: (xl, xh), 0: (xl, xl)}[dx]
+        h = ring if dy else rows
+        w = ring if dx else cols
         f = pl.ds(*fields)
         return pltpu.make_async_remote_copy(
             src_ref=field.at[f, pl.ds(ys[0], h), pl.ds(xs[0], w)],
@@ -139,32 +147,34 @@
             send_sem=send_sem.at[sem], recv_sem=recv_sem.at[sem],
             device_id=device(dy, dx), device_id_type=MESH)
 
-    for slot in range(5):
+    for slot in range(3):
         flip(slot)
-    for n in (2, 1, 0):
-        rows_of(mobility, n, lo, 1, OWN)
-        rows_of(mobility, n, hi - 1, 1, OWN)
-        rows_of(chem, n, lo + 1, rows - 2, INNER)
-
     pl.semaphore_wait(barrier, len(DIRS))
     first = []
     for k, (dy, dx) in enumerate(DIRS):
         if dx == 0:
-            first.append(message(0, k, (0, 2), dy, dx, 2, k))
-            first.append(message(0, k, (2, 1), dy, dx, 1, 8 + k))
+            first.append(message((0, 2), dy, dx, k))
+            first.append(message((2, 1), dy, dx, 32 + k, 1))
         else:
-            first.append(message(0, k, (0, 3), dy, dx, 2, k))
-    later = [message(1, k, (3, 2), dy, dx, 2, 16 + k) for k, (dy, dx) in enumerate(DIRS)]
-    for copy in first + later:
-        copy.start()
+            first.append(message((0, 3), dy, dx, k))
+    for copy in first:
+        copy.start()
+    for slot in range(3, 5):
+        flip(slot)
+    later = [message((3, 2), dy, dx, 8 + k) for k, (dy, dx) in enumerate(DIRS)]
+    for copy in later:
+        copy.start()
+
+    def local(n):
+        rows_of(mobility, n, lo, 2, OWN, rows - 2)
+        rows_of(chem, n, lo + 1, rows - 2, INNER)
 
     def before(n):
         rows_of(gflux, n, lo + 1, rows - 2, CORE)
         rows_of(update, n, lo + 2, rows - 4, MAIN)
 
     def rim(n):
-        rows_of(mobility, n, lo - 2, 1, FULL)
-        rows_of(mobility, n, hi + 1, 1, FULL)
+        rows_of(mobility, n, lo - 2, 2, FULL, rows + 2)
         rows_of(chem, n, lo - 1, 4, FULL, 6)
         rows_of(chem, n, lo + 1, rows - 2, WIDE)
 
@@ -177,12 +187,15 @@
         rows_of(update, n, lo, 4, OWN, 4)
         rows_of(update, n, lo + 2, rows - 4, EDGE)
 
+    local(2)
     before(2)
+    local(1)
+    local(0)
     for copy in first:
         copy.wait_recv()
     rim(2)
     after(2)
-    second = [message(2, k, (5, 1), dy, dx, 2, 24 + k) for k, (dy, dx) in enumerate(DIRS)]
+    second = [message((5, 1), dy, dx, 16 + k) for k, (dy, dx) in enumerate(DIRS)]
     for copy in second:
         copy.start()
     rows_of(grad, 2, lo, rows, ())
@@ -195,7 +208,7 @@
     for copy in second:
         copy.wait_recv()
     after(1)
-    third = [message(3, k, (6, 1), dy, dx, 2, 32 + k) for k, (dy, dx) in enumerate(DIRS)]
+    third = [message((6, 1), dy, dx, 24 + k) for k, (dy, dx) in enumerate(DIRS)]
     for copy in third:
         copy.start()
     before(0)

time: 52.5 us -> 39.1 us (0.74)
  Pallas kernels: 47.7 us -> 34.6 us
    pallas_call x1, Pallas kernels: 47.7 us -> 34.6 us  [shards(): pl.pallas_call(kernel, out_shape=(jax.ShapeDtypeStruct((lanes, rows, cols...]
where the time goes in v1:
time: 39.1 us; the launch traced here: 38.8 us
  Pallas kernels  34.6 us (88%)
  local copies, waits for them, and re-layouts  3.54 us (9%)
  between operations  0.64 us (2%)
    pallas_call x1, Pallas kernels, shards(): pl.pallas_call(kernel, out_shape=(jax.ShapeDtypeStruct((lanes, rows, cols...  34.6 us
    unnamed x2, local copies, waits for them, and re-layouts  3.54 us

profile of v1, /device:TPU:0, one launch (start us, length us, event | category | flops | bytes accessed | tf_op | source)
XLA Modules:
  0.0 38.8 jit_solution(6179392840008950528)
XLA Ops:
  0.6 34.6 %shard_map.50 = (f32[128,8,128]{2,1,0:T(8,128)}, f32[64,8,128]{2,1,0:T(8,128)}) custom-call(f32[3,128,8,128]{3,2,1,0:T(8,128)} %bitcast.3, f32[128,8,128]{2,1,0:T(8,128)} %bitcast.5, f32[64,8,128]{2,1,0:T(8,128)} %refs_2_.1), custom_call_target="tpu_custom_call" | custom-call | tf_op jit(solution)/shard_map/pallas_call | solution.py:250
  35.3 1.9 %copy.7 = f32[2,64,8,128]{3,2,1,0:T(8,128)} copy(f32[2,64,8,128]{3,2,1,0:T(8,128)} %bitcast.4) | data formatting | bytes 1048576
  37.2 1.7 %copy.8 = f32[64,8,128]{2,1,0:T(8,128)} copy(f32[64,8,128]{2,1,0:T(8,128)} %get-tuple-element.9) | data formatting | bytes 524288

commit v2 on v1

--- a/solution.py
+++ b/solution.py
@@ -1,3 +1,5 @@
+import functools
+
 import jax
 import jax.numpy as jnp
 from jax import lax
@@ -12,9 +14,9 @@
 HALO, PAD = 2, 16
 
 
-def body(sizes, conc_hbm, adj_hbm, rate_hbm, out_hbm, grad_hbm,
-         raw, raw_rate, field, mob, pot, inv, gpot, part, acc, outs,
-         load_sem, store_sem, send_sem, recv_sem):
+def body(sizes, conc_hbm, adj_hbm, rate_hbm, last, acc,
+         raw, raw_rate, field, mob, pot, inv, gpot, part,
+         load_sem, send_sem, recv_sem):
     ngx, ngy, rows, cols, depth = sizes
     gx, gy = lax.axis_index("gx"), lax.axis_index("gy")
     lo, hi = HALO, HALO + rows
@@ -101,7 +103,7 @@
             _, lap = laplace(gpot, (), y, x, w)
             new = part[y, pl.ds(x, w)] - lap
             if n == 0:
-                acc[1, y - lo, pl.ds(x - xl, w)] = new
+                last[y - lo, pl.ds(x - xl, w)] = new
             else:
                 field[NEXT[3 - n], y, pl.ds(x, w)] = new
 
@@ -109,8 +111,8 @@
         for x in range(0, cols, 64):
             s = field[NEXT[2 - n], y, pl.ds(xl + x, 64)] * (0.5 - pot[n, y, pl.ds(xl + x, 64)])
             if n < 2:
-                s = s + acc[0, y - lo, pl.ds(x, 64)]
-            acc[0, y - lo, pl.ds(x, 64)] = s
+                s = s + acc[y - lo, pl.ds(x, 64)]
+            acc[y - lo, pl.ds(x, 64)] = s
 
     FULL = ((8, 144),)
     OWN = ((16, 128),)
@@ -213,22 +215,23 @@
         copy.start()
     before(0)
     rows_of(grad, 0, lo, rows, ())
+    for copy in third:
+        copy.wait_recv()
+    after(0)
+    for copy in first + later + second + third:
+        copy.wait_send()
+
+
+def turn(rows, depth, new_ref, sum_ref, out_hbm, grad_hbm, outs, store_sem):
     stores = []
     for y in range(rows):
-        s = acc[0, y]
-        s = 0.1 * (s + pltpu.roll(s, depth, 1))
-        outs[0, y] = s.T
+        outs[1, y] = new_ref[y].T
+        s = sum_ref[y]
+        outs[0, y] = (0.1 * (s + pltpu.roll(s, depth, 1))).T
+        stores.append(pltpu.make_async_copy(outs.at[1, y], out_hbm.at[:, y, :], store_sem.at[1, y]))
         stores.append(pltpu.make_async_copy(outs.at[0, y, pl.ds(0, depth)], grad_hbm.at[:, y, :], store_sem.at[0, y]))
-        stores[-1].start()
-    for copy in third:
-        copy.wait_recv()
-    after(0)
-    for y in range(rows):
-        outs[1, y] = acc[1, y].T
-        stores.append(pltpu.make_async_copy(outs.at[1, y], out_hbm.at[:, y, :], store_sem.at[1, y]))
-        stores[-1].start()
-    for copy in first + later + second + third:
-        copy.wait_send()
+        for copy in stores[-2:]:
+            copy.start()
     for copy in stores:
         copy.wait()
 
@@ -246,12 +249,13 @@
         def kernel(*refs):
             body((ngx, ngy, rows, cols, depth), *refs)
 
-        hbm = pl.BlockSpec(memory_space=pl.ANY)
-        out, grad = pl.pallas_call(
+        hbm = pl.BlockSpec(memory_space=pltpu.HBM)
+        vmem = pl.BlockSpec(memory_space=pltpu.VMEM)
+        tile = jax.ShapeDtypeStruct((rows, cols, lanes), jnp.float32)
+        last, acc = pl.pallas_call(
             kernel,
-            out_shape=(jax.ShapeDtypeStruct((lanes, rows, cols), jnp.float32),
-                       jax.ShapeDtypeStruct((depth, rows, cols), jnp.float32)),
-            in_specs=[hbm] * 3, out_specs=(hbm, hbm),
+            out_shape=(tile, tile),
+            in_specs=[hbm] * 3, out_specs=(vmem, vmem),
             scratch_shapes=[
                 pltpu.VMEM((5, rows, lanes, cols), jnp.float32),
                 pltpu.VMEM((rows, depth, cols), jnp.float32),
@@ -261,16 +265,21 @@
                 pltpu.VMEM((3, *ext), jnp.float32),
                 pltpu.VMEM(ext, jnp.float32),
                 pltpu.VMEM(ext, jnp.float32),
-                pltpu.VMEM((2, rows, cols, lanes), jnp.float32),
-                pltpu.VMEM((2, rows, lanes, cols), jnp.float32),
                 pltpu.SemaphoreType.DMA((5, rows)),
-                pltpu.SemaphoreType.DMA((2, rows)),
                 pltpu.SemaphoreType.DMA((40,)),
                 pltpu.SemaphoreType.DMA((40,)),
             ],
             compiler_params=pltpu.CompilerParams(
-                collective_id=0, has_side_effects=True, vmem_limit_bytes=56 << 20),
-        )(conc, adj, rate_field)
+                collective_id=0, has_side_effects=True, vmem_limit_bytes=48 << 20),
+        )(*(pltpu.with_memory_space_constraint(v, pltpu.HBM) for v in (conc, adj, rate_field)))
+        out, grad = pl.pallas_call(
+            functools.partial(turn, rows, depth),
+            out_shape=(jax.ShapeDtypeStruct((lanes, rows, cols), jnp.float32),
+                       jax.ShapeDtypeStruct((depth, rows, cols), jnp.float32)),
+            in_specs=[vmem, vmem], out_specs=(hbm, hbm),
+            scratch_shapes=[pltpu.VMEM((2, rows, lanes, cols), jnp.float32), pltpu.SemaphoreType.DMA((2, rows))],
+            compiler_params=pltpu.CompilerParams(vmem_limit_bytes=8 << 20),
+        )(last, acc)
         return out.reshape(adjoint_end.shape), grad
 
     return jax.shard_map(

time: 39.1 us -> 35.8 us (0.916)
  local copies, waits for them, and re-layouts: 3.54 us -> 0 us
  Pallas kernels: 34.6 us -> 35 us
    unnamed x2 -> x0, local copies, waits for them, and re-layouts: 3.54 us -> none
    pallas_call x1 -> x2, Pallas kernels: 34.6 us -> 35 us  [the longest x1 33.7 us: shards(): pl.pallas_call(kernel, out_shape=(tile, tile), in_specs=[hbm] * 3, out_sp...]
where the time goes in v2:
time: 35.8 us; the launch traced here: 35.6 us
  Pallas kernels  35 us (98%)
  between operations  0.64 us (2%)
    pallas_call x1, Pallas kernels, shards(): pl.pallas_call(kernel, out_shape=(tile, tile), in_specs=[hbm] * 3, out_sp...  33.7 us
    pallas_call x1, Pallas kernels, shards(): pl.pallas_call(functools.partial(turn, rows, depth), out_shape=(jax.Shape...  1.27 us

profile of v2, /device:TPU:0, one launch (start us, length us, event | category | flops | bytes accessed | tf_op | source)
XLA Modules:
  0.0 35.6 jit_solution(7846268028661915908)
XLA Ops:
  0.6 33.7 %shard_map.50 = (f32[8,128,128]{2,1,0:T(8,128)S(1)}, f32[8,128,128]{2,1,0:T(8,128)S(1)}) custom-call(f32[3,128,8,128]{3,2,1,0:T(8,128)} %bitcast.3, f32[128,8,128]{2,1,0:T(8,128)} %bitcast.4, f32[64,8,128]{2,1,0:T(8,128)} %refs_2_.1), custom_call_target="tpu_custom_call" | custom-call | tf_op jit(solution)/shard_map/pallas_call | solution.py:255
  34.3 1.3 %shard_map.51 = (f32[128,8,128]{2,1,0:T(8,128)}, f32[64,8,128]{2,1,0:T(8,128)}) custom-call(f32[8,128,128]{2,1,0:T(8,128)S(1)} %get-tuple-element.6.new_ref, f32[8,128,128]{2,1,0:T(8,128)S(1)} %get-tuple-element.7.sum_ref), custom_call_target="tpu_custom_call" | custom-call | tf_op jit(solution)/shard_map/pallas_call | solution.py:275

commit v3 on v2

--- a/solution.py
+++ b/solution.py
@@ -149,21 +149,20 @@
             send_sem=send_sem.at[sem], recv_sem=recv_sem.at[sem],
             device_id=device(dy, dx), device_id_type=MESH)
 
-    for slot in range(3):
-        flip(slot)
+    flip(0)
+    flip(1)
     pl.semaphore_wait(barrier, len(DIRS))
-    first = []
-    for k, (dy, dx) in enumerate(DIRS):
-        if dx == 0:
-            first.append(message((0, 2), dy, dx, k))
-            first.append(message((2, 1), dy, dx, 32 + k, 1))
-        else:
-            first.append(message((0, 3), dy, dx, k))
+    first = [message((0, 2), dy, dx, k) for k, (dy, dx) in enumerate(DIRS)]
     for copy in first:
         copy.start()
+    flip(RATE)
+    rates = [message((RATE, 1), dy, dx, 28 + k, 1) for k, (dy, dx) in enumerate(DIRS) if not (dy and dx)]
+    for copy in rates:
+        copy.start()
+    first += rates
     for slot in range(3, 5):
         flip(slot)
-    later = [message((3, 2), dy, dx, 8 + k) for k, (dy, dx) in enumerate(DIRS)]
+    later = [message((3, 1), dy, dx, 8 + k) for k, (dy, dx) in enumerate(DIRS)]
     for copy in later:
         copy.start()
 
@@ -200,12 +199,14 @@
     second = [message((5, 1), dy, dx, 16 + k) for k, (dy, dx) in enumerate(DIRS)]
     for copy in second:
         copy.start()
+    late = [message((4, 1), dy, dx, 40 + k) for k, (dy, dx) in enumerate(DIRS)]
+    for copy in late:
+        copy.start()
     rows_of(grad, 2, lo, rows, ())
     for copy in later:
         copy.wait_recv()
     rim(1)
     before(1)
-    rim(0)
     rows_of(grad, 1, lo, rows, ())
     for copy in second:
         copy.wait_recv()
@@ -213,12 +214,15 @@
     third = [message((6, 1), dy, dx, 24 + k) for k, (dy, dx) in enumerate(DIRS)]
     for copy in third:
         copy.start()
+    for copy in late:
+        copy.wait_recv()
+    rim(0)
     before(0)
     rows_of(grad, 0, lo, rows, ())
     for copy in third:
         copy.wait_recv()
     after(0)
-    for copy in first + later + second + third:
+    for copy in first + later + late + second + third:
         copy.wait_send()
 
 
@@ -266,8 +270,8 @@
                 pltpu.VMEM(ext, jnp.float32),
                 pltpu.VMEM(ext, jnp.float32),
                 pltpu.SemaphoreType.DMA((5, rows)),
-                pltpu.SemaphoreType.DMA((40,)),
-                pltpu.SemaphoreType.DMA((40,)),
+                pltpu.SemaphoreType.DMA((48,)),
+                pltpu.SemaphoreType.DMA((48,)),
             ],
             compiler_params=pltpu.CompilerParams(
                 collective_id=0, has_side_effects=True, vmem_limit_bytes=48 << 20),

time: 35.8 us -> 33.8 us (0.944)
  Pallas kernels: 35 us -> 33 us
    pallas_call x1, Pallas kernels: 33.7 us -> 31.7 us  [shards(): pl.pallas_call(kernel, out_shape=(tile, tile), in_specs=[hbm] * 3, out_sp...]
where the time goes in v3:
time: 33.8 us; the launch traced here: 33.6 us
  Pallas kernels  33 us (98%)
  between operations  0.64 us (2%)
    pallas_call x1, Pallas kernels, shards(): pl.pallas_call(kernel, out_shape=(tile, tile), in_specs=[hbm] * 3, out_sp...  31.7 us
    pallas_call x1, Pallas kernels, shards(): pl.pallas_call(functools.partial(turn, rows, depth), out_shape=(jax.Shape...  1.27 us

profile of v3, /device:TPU:0, one launch (start us, length us, event | category | flops | bytes accessed | tf_op | source)
XLA Modules:
  0.0 33.6 jit_solution(9933695585491073482)
XLA Ops:
  0.6 31.7 %shard_map.50 = (f32[8,128,128]{2,1,0:T(8,128)S(1)}, f32[8,128,128]{2,1,0:T(8,128)S(1)}) custom-call(f32[3,128,8,128]{3,2,1,0:T(8,128)} %bitcast.3, f32[128,8,128]{2,1,0:T(8,128)} %bitcast.4, f32[64,8,128]{2,1,0:T(8,128)} %refs_2_.1), custom_call_target="tpu_custom_call" | custom-call | tf_op jit(solution)/shard_map/pallas_call | solution.py:259
  32.4 1.3 %shard_map.51 = (f32[128,8,128]{2,1,0:T(8,128)}, f32[64,8,128]{2,1,0:T(8,128)}) custom-call(f32[8,128,128]{2,1,0:T(8,128)S(1)} %get-tuple-element.6.new_ref, f32[8,128,128]{2,1,0:T(8,128)S(1)} %get-tuple-element.7.sum_ref), custom_call_target="tpu_custom_call" | custom-call | tf_op jit(solution)/shard_map/pallas_call | solution.py:279

commit v4 on v3

--- a/solution.py
+++ b/solution.py
@@ -14,8 +14,8 @@
 HALO, PAD = 2, 16
 
 
-def body(sizes, conc_hbm, adj_hbm, rate_hbm, last, acc,
-         raw, raw_rate, field, mob, pot, inv, gpot, part,
+def body(sizes, conc_hbm, adj_hbm, rate_hbm, last, turned,
+         raw, raw_rate, acc, field, mob, pot, inv, gpot, part,
          load_sem, send_sem, recv_sem):
     ngx, ngy, rows, cols, depth = sizes
     gx, gy = lax.axis_index("gx"), lax.axis_index("gy")
@@ -190,8 +190,6 @@
 
     local(2)
     before(2)
-    local(1)
-    local(0)
     for copy in first:
         copy.wait_recv()
     rim(2)
@@ -203,6 +201,7 @@
     for copy in late:
         copy.start()
     rows_of(grad, 2, lo, rows, ())
+    local(1)
     for copy in later:
         copy.wait_recv()
     rim(1)
@@ -214,11 +213,15 @@
     third = [message((6, 1), dy, dx, 24 + k) for k, (dy, dx) in enumerate(DIRS)]
     for copy in third:
         copy.start()
+    local(0)
     for copy in late:
         copy.wait_recv()
     rim(0)
     before(0)
     rows_of(grad, 0, lo, rows, ())
+    for y in range(rows):
+        s = acc[y]
+        turned[y] = (0.1 * (s + pltpu.roll(s, depth, 1))).T[:depth]
     for copy in third:
         copy.wait_recv()
     after(0)
@@ -226,16 +229,15 @@
         copy.wait_send()
 
 
-def turn(rows, depth, new_ref, sum_ref, out_hbm, grad_hbm, outs, store_sem):
+def turn(rows, new_ref, grad_ref, out_hbm, grad_hbm, outs, store_sem):
     stores = []
     for y in range(rows):
-        outs[1, y] = new_ref[y].T
-        s = sum_ref[y]
-        outs[0, y] = (0.1 * (s + pltpu.roll(s, depth, 1))).T
-        stores.append(pltpu.make_async_copy(outs.at[1, y], out_hbm.at[:, y, :], store_sem.at[1, y]))
-        stores.append(pltpu.make_async_copy(outs.at[0, y, pl.ds(0, depth)], grad_hbm.at[:, y, :], store_sem.at[0, y]))
-        for copy in stores[-2:]:
-            copy.start()
+        stores.append(pltpu.make_async_copy(grad_ref.at[y], grad_hbm.at[:, y, :], store_sem.at[0, y]))
+        stores[-1].start()
+    for y in range(rows):
+        outs[y] = new_ref[y].T
+        stores.append(pltpu.make_async_copy(outs.at[y], out_hbm.at[:, y, :], store_sem.at[1, y]))
+        stores[-1].start()
     for copy in stores:
         copy.wait()
 
@@ -255,14 +257,15 @@
 
         hbm = pl.BlockSpec(memory_space=pltpu.HBM)
         vmem = pl.BlockSpec(memory_space=pltpu.VMEM)
-        tile = jax.ShapeDtypeStruct((rows, cols, lanes), jnp.float32)
-        last, acc = pl.pallas_call(
+        last, grad = pl.pallas_call(
             kernel,
-            out_shape=(tile, tile),
+            out_shape=(jax.ShapeDtypeStruct((rows, cols, lanes), jnp.float32),
+                       jax.ShapeDtypeStruct((rows, depth, cols), jnp.float32)),
             in_specs=[hbm] * 3, out_specs=(vmem, vmem),
             scratch_shapes=[
                 pltpu.VMEM((5, rows, lanes, cols), jnp.float32),
                 pltpu.VMEM((rows, depth, cols), jnp.float32),
+                pltpu.VMEM((rows, cols, lanes), jnp.float32),
                 pltpu.VMEM((7, *ext), jnp.float32),
                 pltpu.VMEM((3, *ext), jnp.float32),
                 pltpu.VMEM((3, *ext), jnp.float32),
@@ -277,13 +280,13 @@
                 collective_id=0, has_side_effects=True, vmem_limit_bytes=48 << 20),
         )(*(pltpu.with_memory_space_constraint(v, pltpu.HBM) for v in (conc, adj, rate_field)))
         out, grad = pl.pallas_call(
-            functools.partial(turn, rows, depth),
+            functools.partial(turn, rows),
             out_shape=(jax.ShapeDtypeStruct((lanes, rows, cols), jnp.float32),
                        jax.ShapeDtypeStruct((depth, rows, cols), jnp.float32)),
             in_specs=[vmem, vmem], out_specs=(hbm, hbm),
-            scratch_shapes=[pltpu.VMEM((2, rows, lanes, cols), jnp.float32), pltpu.SemaphoreType.DMA((2, rows))],
+            scratch_shapes=[pltpu.VMEM((rows, lanes, cols), jnp.float32), pltpu.SemaphoreType.DMA((2, rows))],
             compiler_params=pltpu.CompilerParams(vmem_limit_bytes=8 << 20),
-        )(last, acc)
+        )(last, grad)
         return out.reshape(adjoint_end.shape), grad
 
     return jax.shard_map(

time: 33.8 us -> 33.5 us (level)
  no operation moved by 1% of the time
where the time goes in v4:
time: 33.5 us; the launch traced here: 33.4 us
  Pallas kernels  32.7 us (98%)
  between operations  0.64 us (2%)
    pallas_call x1, Pallas kernels, shards(): pl.pallas_call(kernel, out_shape=(jax.ShapeDtypeStruct((rows, cols, lanes...  31.7 us
    pallas_call x1, Pallas kernels, shards(): pl.pallas_call(functools.partial(turn, rows), out_shape=(jax.ShapeDtypeSt...  1.02 us

profile of v4, /device:TPU:0, one launch (start us, length us, event | category | flops | bytes accessed | tf_op | source)
XLA Modules:
  0.0 33.4 jit_solution(15410930288622188183)
XLA Ops:
  0.6 31.7 %shard_map.50 = (f32[8,128,128]{2,1,0:T(8,128)S(1)}, f32[8,64,128]{2,1,0:T(8,128)S(1)}) custom-call(f32[3,128,8,128]{3,2,1,0:T(8,128)} %bitcast.3, f32[128,8,128]{2,1,0:T(8,128)} %bitcast.4, f32[64,8,128]{2,1,0:T(8,128)} %refs_2_.1), custom_call_target="tpu_custom_call" | custom-call | tf_op jit(solution)/shard_map/pallas_call | solution.py:260
  32.4 1.0 %shard_map.51 = (f32[128,8,128]{2,1,0:T(8,128)}, f32[64,8,128]{2,1,0:T(8,128)}) custom-call(f32[8,128,128]{2,1,0:T(8,128)S(1)} %get-tuple-element.6.new_ref, f32[8,64,128]{2,1,0:T(8,128)S(1)} %get-tuple-element.7.grad_ref), custom_call_target="tpu_custom_call" | custom-call | tf_op jit(solution)/shard_map/pallas_call | solution.py:282

commit v5 on v4

--- a/solution.py
+++ b/solution.py
@@ -179,13 +179,18 @@
         rows_of(chem, n, lo - 1, 4, FULL, 6)
         rows_of(chem, n, lo + 1, rows - 2, WIDE)
 
-    def after(n):
+    def after(n, corners=()):
         if n == 2:
             rows_of(gflux, n, lo - 1, 6, FULL, 4)
         else:
             rows_of(gflux, n, lo - 1, 4, FULL, 6)
-        rows_of(gflux, n, lo + 1, rows - 2, WIDE)
-        rows_of(update, n, lo, 4, OWN, 4)
+            rows_of(gflux, n, lo + 1, rows - 2, WIDE)
+        rows_of(update, n, lo, 2, OWN, rows - 2)
+        for copy in corners:
+            copy.start()
+        if n == 2:
+            rows_of(gflux, n, lo + 1, rows - 2, WIDE)
+        rows_of(update, n, lo + 1, 2, OWN, rows - 4)
         rows_of(update, n, lo + 2, rows - 4, EDGE)
 
     local(2)
@@ -193,9 +198,9 @@
     for copy in first:
         copy.wait_recv()
     rim(2)
-    after(2)
     second = [message((5, 1), dy, dx, 16 + k) for k, (dy, dx) in enumerate(DIRS)]
-    for copy in second:
+    after(2, second[:4])
+    for copy in second[4:]:
         copy.start()
     late = [message((4, 1), dy, dx, 40 + k) for k, (dy, dx) in enumerate(DIRS)]
     for copy in late:
@@ -209,9 +214,9 @@
     rows_of(grad, 1, lo, rows, ())
     for copy in second:
         copy.wait_recv()
-    after(1)
     third = [message((6, 1), dy, dx, 24 + k) for k, (dy, dx) in enumerate(DIRS)]
-    for copy in third:
+    after(1, third[:4])
+    for copy in third[4:]:
         copy.start()
     local(0)
     for copy in late:

time: 33.5 us -> 33.5 us (level)
  no operation moved by 1% of the time
where the time goes in v5:
time: 33.5 us; the launch traced here: 33.4 us
  Pallas kernels  32.7 us (98%)
  between operations  0.64 us (2%)
    pallas_call x1, Pallas kernels, shards(): pl.pallas_call(kernel, out_shape=(jax.ShapeDtypeStruct((rows, cols, lanes...  31.7 us
    pallas_call x1, Pallas kernels, shards(): pl.pallas_call(functools.partial(turn, rows), out_shape=(jax.ShapeDtypeSt...  1.02 us

profile of v5, /device:TPU:0, one launch (start us, length us, event | category | flops | bytes accessed | tf_op | source)
XLA Modules:
  0.0 33.4 jit_solution(6231933891699065990)
XLA Ops:
  0.6 31.7 %shard_map.50 = (f32[8,128,128]{2,1,0:T(8,128)S(1)}, f32[8,64,128]{2,1,0:T(8,128)S(1)}) custom-call(f32[3,128,8,128]{3,2,1,0:T(8,128)} %bitcast.3, f32[128,8,128]{2,1,0:T(8,128)} %bitcast.4, f32[64,8,128]{2,1,0:T(8,128)} %refs_2_.1), custom_call_target="tpu_custom_call" | custom-call | tf_op jit(solution)/shard_map/pallas_call | solution.py:265
  32.3 1.0 %shard_map.51 = (f32[128,8,128]{2,1,0:T(8,128)}, f32[64,8,128]{2,1,0:T(8,128)}) custom-call(f32[8,128,128]{2,1,0:T(8,128)S(1)} %get-tuple-element.6.new_ref, f32[8,64,128]{2,1,0:T(8,128)S(1)} %get-tuple-element.7.grad_ref), custom_call_target="tpu_custom_call" | custom-call | tf_op jit(solution)/shard_map/pallas_call | solution.py:287
